TPU v7x, 32 devices: a whole 2x2x4 slice. The times are simulated.
32 devices in a mesh: group: 8 (over z, x), member: 4 (over y, core).
Axes of the slice: x: 2, y: 2, z: 4, core: 2. Of those that a mesh axis runs over, the one named last changes fastest.
Arguments:
- particles: float32 [8, 65536], P(None, ('group', 'member')), may hold values from 0 to 20, as said below
- new_slot: int32 [512], P(('group', 'member')), may hold values from 0 to 511, as said below
- neighbours: int32 [512, 6], P(('group', 'member')), may hold values from 0 to 23, as said below
- ghosts: int32 [32, 2], P(('group', 'member')), may hold values from 0 to 4, as said below
Outputs:
- energy: float32 [65536], P(('group', 'member'))
- density: float32 [65536], P(('group', 'member'))
Inputs may be any that keep to these rules, and one draw needn't show every extreme that they name: A permutation of 0 to 511. Tile t goes to segment new_slot[t] // 16, where segment number = group index * 4 + member index; a tile keeps its member index. Every segment receives 16 tiles, no segment sends more than 4 tiles to one segment, and some segment sends exactly 4 tiles to one segment. `ghosts`: row d holds the number of tiles that segment d takes from the end of segment d - 1 and from the start of segment d + 1. Both are at least 1 except the first segment's left count and the last segment's right count, which are 0; some segment takes exactly 4 tiles from its left neighbour. `neighbours`: for moved tile s of segment d, entries count along the extended range: the last ghosts[d, 0] tiles of segment d - 1, then the 16 tiles of segment d, then the first ghosts[d, 1] tiles of segment d + 1; every entry lies inside that range, entry 0 is the tile itself, and entries may repeat. `particles`: Rows: positions within 0 to 1, masses within 0.5 / 768 to 2 / 768, smoothing lengths within 0.3 to 0.5, initial energies within 0.5 to 4, opacities within 0.05 to 20, heating within 0 to 1.
All inputs are finite; a program needn't handle non-finite values.
Results may differ from a plain program's by a relative error of at most 0.00014.
Values sent between devices are 32-bit elements; how exact they have to be, the bound alone decides.
A program may use at most 64 MiB of HBM per device.

v0:
```python
import math

import jax
import jax.numpy as jnp
from jax import lax
from jax.sharding import PartitionSpec as P

TILE = 128
GMAX = 4
SWEEPS = 3


KERNEL_NORM = 21.0 / (16.0 * math.pi)
TIME_STEP = 0.05


def shifted(value, axis, steps):
    count = lax.axis_size(axis)
    first, last = (max(0, -steps), min(count, count - steps))
    return lax.ppermute(value, axis, [(source, source + steps) for source in range(first, last)])


def geometry(own_fields, near_fields):
    offsets = near_fields[0:3, :, :, None, :] - own_fields[0:3, :, None, :, None]
    distance = jnp.sqrt(jnp.sum(offsets * offsets, axis=0))
    return (offsets, distance)


def pair_forces(own_fields, near_fields, distance):
    mean_smooth = 0.5 * (own_fields[4][:, None, :, None] + near_fields[4][:, :, None, :])
    falloff = jax.nn.relu(1.0 - 0.5 * distance / mean_smooth)
    return 5.0 * KERNEL_NORM * falloff**3 / mean_smooth**5


def density_kernel(own_items, near_items):
    own_fields = own_items[0]
    near_fields = near_items[0]
    offsets, distance = geometry(own_fields, near_fields)
    smooth = own_fields[4][:, None, :, None]
    scaled = distance / smooth
    falloff = jax.nn.relu(1.0 - 0.5 * scaled)
    weight = KERNEL_NORM * falloff**4 * (2.0 * scaled + 1.0) / smooth**3
    return jnp.sum(near_fields[3][:, :, None, :] * weight, axis=(1, 3))


def limiter_kernel(own_items, near_items):
    own_fields, own_density, own_energy = own_items
    near_fields, near_density, near_energy = near_items
    offsets, distance = geometry(own_fields, near_fields)
    forces = pair_forces(own_fields, near_fields, distance)
    volume = near_fields[3] / near_density[0]
    change = near_energy[0][:, :, None, :] - own_energy[0][:, None, :, None]
    scaled = volume[:, :, None, :] * forces * change
    gradient = jnp.sum(scaled[None] * offsets, axis=(2, 4))
    stream_ratio = jnp.sqrt(jnp.sum(gradient * gradient, axis=0)) / (
        own_fields[6] * own_density[0] * own_energy[0]
    )
    limiter = (2.0 + stream_ratio) / (6.0 + 3.0 * stream_ratio + stream_ratio * stream_ratio)
    return limiter / (own_fields[6] * own_density[0])


def jacobi_kernel(own_items, near_items):
    own_fields, own_density, own_diffusion = own_items
    near_fields, near_density, near_diffusion, near_energy = near_items
    offsets, distance = geometry(own_fields, near_fields)
    forces = pair_forces(own_fields, near_fields, distance)
    coupling = (
        near_fields[3][:, :, None, :]
        * (own_diffusion[0][:, None, :, None] + near_diffusion[0][:, :, None, :])
        * forces
    )
    coupling = coupling / (own_density[0][:, None, :, None] * near_density[0][:, :, None, :])
    rate_sum = jnp.sum(coupling, axis=(1, 3))
    inflow = jnp.sum(coupling * near_energy[0][:, :, None, :], axis=(1, 3))
    return (own_fields[5] + TIME_STEP * own_fields[7] + TIME_STEP * inflow) / (
        1.0 + TIME_STEP * rate_sum
    )


def tile_blocks(kernel, own_items, ext_items, near_index):
    per_block = 4
    block_count = near_index.shape[0] // per_block

    def one_block(block_id):
        first_tile = block_id * per_block
        own_part = tuple(
            (lax.dynamic_slice_in_dim(values, first_tile, per_block, 1) for values in own_items)
        )
        near_rows = lax.dynamic_slice_in_dim(near_index, first_tile, per_block, 0)
        near_part = tuple((jnp.take(values, near_rows, axis=1) for values in ext_items))
        return kernel(own_part, near_part)

    blocks = lax.map(one_block, jnp.arange(block_count, dtype=jnp.int32))
    return blocks.reshape(1, near_index.shape[0], blocks.shape[-1])


def with_ghosts(values, depth_tiles):
    tail_rows = values[:, values.shape[1] - depth_tiles :]
    head_rows = values[:, :depth_tiles]
    from_left = shifted(tail_rows, ("group", "member"), 1)
    from_right = shifted(head_rows, ("group", "member"), -1)
    return jnp.concatenate([from_left, values, from_right], axis=1)


def local(particles, new_slot, neighbours, ghosts):
    tile_count = new_slot.shape[0]
    local_tiles = particles.reshape(8, tile_count, TILE)
    groups = lax.axis_size("group")
    members = lax.axis_size("member")
    capacity = max(2, (2 * tile_count + groups - 1) // groups)
    target = new_slot // (tile_count * members)
    in_group = (target[:, None] == jnp.arange(groups, dtype=jnp.int32)[None, :]).astype(jnp.int32)
    order_in = jnp.sum(jnp.cumsum(in_group, axis=0) * in_group, axis=1) - 1
    bucket = target * capacity + order_in
    placement = bucket[:, None] == jnp.arange(groups * capacity, dtype=jnp.int32)[None, :]
    outgoing = jnp.einsum(
        "ts,kti->ski", placement.astype(jnp.float32), local_tiles, precision=lax.Precision.HIGHEST
    )
    slot_label = new_slot % tile_count + 1
    out_slots = jnp.sum(placement.astype(jnp.int32) * slot_label[:, None], axis=0)
    received, got_slots = (
        lax.all_to_all(outgoing, "group", split_axis=0, concat_axis=0, tiled=True),
        lax.all_to_all(out_slots, "group", split_axis=0, concat_axis=0, tiled=True),
    )
    choose = (got_slots[:, None] - 1 == jnp.arange(tile_count, dtype=jnp.int32)[None, :]).astype(
        jnp.float32
    )
    arranged = jnp.einsum("st,ski->kti", choose, received, precision=lax.Precision.HIGHEST)
    left_count = ghosts[0, 0]
    near_index = neighbours + (GMAX - left_count)
    statics = with_ghosts(arranged[0:6], GMAX)
    density = tile_blocks(density_kernel, (arranged,), (statics,), near_index)
    density_ext = with_ghosts(density, GMAX)
    energy = arranged[5:6]
    energy_ext = statics[5:6]
    for sweep_step in range(SWEEPS):
        if sweep_step > 0:
            energy_ext = with_ghosts(energy, GMAX)
        diffusion = tile_blocks(
            limiter_kernel,
            (arranged, density, energy),
            (statics, density_ext, energy_ext),
            near_index,
        )
        diffusion_ext = with_ghosts(diffusion, GMAX)
        energy = tile_blocks(
            jacobi_kernel,
            (arranged, density, diffusion),
            (statics, density_ext, diffusion_ext, energy_ext),
            near_index,
        )
    return (energy.reshape(-1), density.reshape(-1))


def solution(mesh):
    in_specs = (
        P(None, ("group", "member")),
        P(("group", "member")),
        P(("group", "member"), None),
        P(("group", "member"), None),
    )
    out_specs = (P(("group", "member")), P(("group", "member")))
    return jax.shard_map(local, mesh=mesh, in_specs=in_specs, out_specs=out_specs, check_vma=False)
```

profile of v0, /device:TPU:7, one launch (start us, length us, event | category | flops | bytes accessed | tf_op | source)
XLA Modules:
  0.0 254.7 jit_solution(4087296873191726330)
XLA Ops:
  2.4 5.8 %all-to-all-start.1 = ((s32[8,4,1]{1,2,0:T(1,128)}), s32[8,4,1]{1,2,0:T(1,128)S(1)}, u32[]{:S(2)}, u32[]{:S(2)}) async-start(s32[8,4,1]{1,2,0:T(1,128)} %bitcast.89), calls=%async_computation.1 | async-start | bytes 8192 | tf_op jit(solution)/shard_map/all_to_all | solution.py:123
  9.2 3.0 %all-to-all-done.1 = s32[8,4,1]{1,2,0:T(1,128)S(1)} async-done(((s32[8,4,1]{1,2,0:T(1,128)}), s32[8,4,1]{1,2,0:T(1,128)S(1)}, u32[]{:S(2)}, u32[]{:S(2)}) %all-to-all-start.1) | async-done | bytes 160 | tf_op jit(solution)/shard_map/all_to_all | solution.py:123
  12.3 4.5 %all-to-all-start = ((f32[32,8,128]{2,1,0:T(8,128)}), f32[32,8,128]{2,1,0:T(8,128)S(1)}, u32[]{:S(2)}, u32[]{:S(2)}) async-start(f32[32,8,128]{2,1,0:T(8,128)} %copy.49), calls=%async_computation | async-start | bytes 262144 | tf_op jit(solution)/shard_map/all_to_all | solution.py:122
  18.3 3.2 %all-to-all-done = f32[32,8,128]{2,1,0:T(8,128)S(1)} async-done(((f32[32,8,128]{2,1,0:T(8,128)}), f32[32,8,128]{2,1,0:T(8,128)S(1)}, u32[]{:S(2)}, u32[]{:S(2)}) %all-to-all-start) | async-done | bytes 131104 | tf_op jit(solution)/shard_map/all_to_all | solution.py:122
  21.6 5.8 %collective-permute-start = (f32[6,4,128]{2,1,0:T(4,128)S(1)}, f32[6,4,128]{2,1,0:T(4,128)S(1)}, u32[]{:S(2)}, u32[]{:S(2)}) collective-permute-start(f32[6,4,128]{2,1,0:T(4,128)S(1)} %get-tuple-element.782), channel_id=1, source_target_pairs={{0,1},{1,2},{2,3},{3,4},{4,5},{5,6},{6,7},{7,8},{8,9},{9,10},{10,1... | collective-permute-start | bytes 36872 | tf_op jit(solution)/shard_map/ppermute | solution.py:20
  27.5 1.9 collective-permute-start.1
  29.4 4.8 %collective-permute-done.1 = f32[6,4,128]{2,1,0:T(4,128)S(1)} collective-permute-done((f32[6,4,128]{2,1,0:T(4,128)S(1)}, f32[6,4,128]{2,1,0:T(4,128)S(1)}, u32[]{:S(2)}, u32[]{:S(2)}) %collective-permute-start.1) | collective-permute-done | bytes 12320 | tf_op jit(solution)/shard_map/ppermute | solution.py:20
  34.3 15.3 %while.70 = (s32[]{:T(128)}, f32[4,4,128]{2,1,0:T(4,128)S(1)}, s32[4]{0:T(128)S(1)}, s32[16,6]{1,0:T(8,128)S(1)}, f32[6,24,128]{2,0,1:T(8,128)S(1)}, /*index=5*/...) while((s32[]{:T(128)}, f32[4,4,128]{2,1,0:T(4,128)S(1)}, ...), condition=%wide.region_6.8_spmd, body=%wide.region_3.7_spmd.sunk | while | flops 8277655 | bytes 3627839 | solution.py:93
  49.7 1.9 collective-permute-start.2
  51.6 2.4 collective-permute-start.3
  54.0 4.3 %collective-permute-done.3 = f32[1,4,128]{2,1,0:T(4,128)S(1)} collective-permute-done((f32[1,4,128]{2,1,0:T(4,128)S(1)}, f32[1,4,128]{2,1,0:T(4,128)S(1)}, u32[]{:S(2)}, u32[]{:S(2)}) %collective-permute-start.3) | collective-permute-done | bytes 2080 | tf_op jit(solution)/shard_map/ppermute | solution.py:20
  58.3 24.6 %while.71 = (s32[]{:T(128)}, f32[4,4,128]{2,1,0:T(4,128)S(1)}, s32[4]{0:T(128)S(1)}, s32[16,6]{1,0:T(8,128)S(1)}, f32[6,24,128]{2,0,1:T(8,128)S(1)}, /*index=5*/...) while((s32[]{:T(128)}, f32[4,4,128]{2,1,0:T(4,128)S(1)}, ...), condition=%wide.region_11.14_spmd, body=%wide.region_7.13_spmd.sunk | while | flops 13011096 | bytes 7021651 | solution.py:93
  83.0 2.0 collective-permute-start.4
  85.0 2.4 collective-permute-start.5
  87.3 4.3 %collective-permute-done.5 = f32[1,4,128]{2,1,0:T(4,128)S(1)} collective-permute-done((f32[1,4,128]{2,1,0:T(4,128)S(1)}, f32[1,4,128]{2,1,0:T(4,128)S(1)}, u32[]{:S(2)}, u32[]{:S(2)}) %collective-permute-start.5) | collective-permute-done | bytes 2080 | tf_op jit(solution)/shard_map/ppermute | solution.py:20
  91.7 26.1 %while.72 = (s32[]{:T(128)}, f32[4,4,128]{2,1,0:T(4,128)S(1)}, s32[4]{0:T(128)S(1)}, f32[8,16,128]{2,1,0:T(8,128)S(1)}, s32[16,6]{1,0:T(8,128)S(1)}, /*index=5*/...) while((s32[]{:T(128)}, f32[4,4,128]{2,1,0:T(4,128)S(1)}, ...), condition=%wide.region_16.19_spmd, body=%wide.region_12.18_spmd.sunk | while | flops 11434649 | bytes 3939543 | solution.py:93
  96.1 2.0 multiply_reduce_fusion.26
  102.7 2.0 multiply_reduce_fusion.26
  109.2 2.0 multiply_reduce_fusion.26
  115.7 2.0 multiply_reduce_fusion.26
  117.8 2.0 collective-permute-start.6
  119.8 2.6 %collective-permute-start.7 = (f32[1,4,128]{2,1,0:T(4,128)S(1)}, f32[1,4,128]{2,1,0:T(4,128)S(1)}, u32[]{:S(2)}, u32[]{:S(2)}) collective-permute-start(f32[1,4,128]{2,1,0:T(4,128)S(1)} %get-tuple-element.791), channel_id=1, source_target_pairs={{1,0},{2,1},{3,2},{4,3},{5,4},{6,5},{7,6},{8,7},{9,8},{10,9},{11,1... | collective-permute-start | bytes 6152 | tf_op jit(solution)/shard_map/ppermute | solution.py:20
  122.3 4.1 %collective-permute-done.7 = f32[1,4,128]{2,1,0:T(4,128)S(1)} collective-permute-done((f32[1,4,128]{2,1,0:T(4,128)S(1)}, f32[1,4,128]{2,1,0:T(4,128)S(1)}, u32[]{:S(2)}, u32[]{:S(2)}) %collective-permute-start.7) | collective-permute-done | bytes 2080 | tf_op jit(solution)/shard_map/ppermute | solution.py:20
  126.5 24.6 %while.73 = (s32[]{:T(128)}, f32[4,4,128]{2,1,0:T(4,128)S(1)}, s32[4]{0:T(128)S(1)}, s32[16,6]{1,0:T(8,128)S(1)}, f32[6,24,128]{2,0,1:T(8,128)S(1)}, /*index=5*/...) while((s32[]{:T(128)}, f32[4,4,128]{2,1,0:T(4,128)S(1)}, ...), condition=%wide.region_21.24_spmd, body=%wide.region_17.23_spmd.sunk | while | flops 13011096 | bytes 7021651 | solution.py:93
  130.4 1.4 fusion.106
  136.5 1.4 fusion.106
  142.7 1.4 fusion.106
  148.8 1.4 fusion.106
  151.1 2.0 collective-permute-start.8
  153.1 2.4 collective-permute-start.9
  155.5 4.3 %collective-permute-done.9 = f32[1,4,128]{2,1,0:T(4,128)S(1)} collective-permute-done((f32[1,4,128]{2,1,0:T(4,128)S(1)}, f32[1,4,128]{2,1,0:T(4,128)S(1)}, u32[]{:S(2)}, u32[]{:S(2)}) %collective-permute-start.9) | collective-permute-done | bytes 2080 | tf_op jit(solution)/shard_map/ppermute | solution.py:20
  159.8 26.1 %while.74 = (s32[]{:T(128)}, f32[4,4,128]{2,1,0:T(4,128)S(1)}, s32[4]{0:T(128)S(1)}, f32[8,16,128]{2,1,0:T(8,128)S(1)}, s32[16,6]{1,0:T(8,128)S(1)}, /*index=5*/...) while((s32[]{:T(128)}, f32[4,4,128]{2,1,0:T(4,128)S(1)}, ...), condition=%wide.region_26.29_spmd, body=%wide.region_22.28_spmd.sunk | while | flops 11434649 | bytes 3939543 | solution.py:93
  164.3 2.0 multiply_reduce_fusion.29
  170.8 2.0 multiply_reduce_fusion.29
  177.3 2.0 multiply_reduce_fusion.29
  183.9 2.0 multiply_reduce_fusion.29
  185.9 2.0 collective-permute-start.10
  187.9 2.4 collective-permute-start.11
  190.3 4.3 %collective-permute-done.11 = f32[1,4,128]{2,1,0:T(4,128)S(1)} collective-permute-done((f32[1,4,128]{2,1,0:T(4,128)S(1)}, f32[1,4,128]{2,1,0:T(4,128)S(1)}, u32[]{:S(2)}, u32[]{:S(2)}) %collective-permute-start.11) | collective-permute-done | bytes 2080 | tf_op jit(solution)/shard_map/ppermute | solution.py:20
  194.6 24.6 %while.75 = (s32[]{:T(128)}, f32[4,4,128]{2,1,0:T(4,128)S(1)}, s32[4]{0:T(128)S(1)}, s32[16,6]{1,0:T(8,128)S(1)}, f32[6,24,128]{2,0,1:T(8,128)S(1)}, /*index=5*/...) while((s32[]{:T(128)}, f32[4,4,128]{2,1,0:T(4,128)S(1)}, ...), condition=%wide.region_31.34_spmd, body=%wide.region_27.33_spmd.sunk | while | flops 13011096 | bytes 7021651 | solution.py:93
  219.3 2.0 collective-permute-start.12
  221.2 2.6 %collective-permute-start.13 = (f32[1,4,128]{2,1,0:T(4,128)S(1)}, f32[1,4,128]{2,1,0:T(4,128)S(1)}, u32[]{:S(2)}, u32[]{:S(2)}) collective-permute-start(f32[1,4,128]{2,1,0:T(4,128)S(1)} %get-tuple-element.785), channel_id=1, source_target_pairs={{1,0},{2,1},{3,2},{4,3},{5,4},{6,5},{7,6},{8,7},{9,8},{10,9},{11,1... | collective-permute-start | bytes 6152 | tf_op jit(solution)/shard_map/ppermute | solution.py:20
  223.9 4.1 %collective-permute-done.13 = f32[1,4,128]{2,1,0:T(4,128)S(1)} collective-permute-done((f32[1,4,128]{2,1,0:T(4,128)S(1)}, f32[1,4,128]{2,1,0:T(4,128)S(1)}, u32[]{:S(2)}, u32[]{:S(2)}) %collective-permute-start.13) | collective-permute-done | bytes 2080 | tf_op jit(solution)/shard_map/ppermute | solution.py:20
  228.0 26.1 %while.76 = (s32[]{:T(128)}, f32[4,4,128]{2,1,0:T(4,128)S(1)}, s32[4]{0:T(128)S(1)}, f32[8,16,128]{2,1,0:T(8,128)S(1)}, s32[16,6]{1,0:T(8,128)S(1)}, /*index=5*/...) while((s32[]{:T(128)}, f32[4,4,128]{2,1,0:T(4,128)S(1)}, ...), condition=%wide.region_36.39_spmd, body=%wide.region_32.38_spmd.sunk | while | flops 11434649 | bytes 3939543 | solution.py:93
  232.4 2.0 multiply_reduce_fusion.32
  239.0 2.0 multiply_reduce_fusion.32
  245.5 2.0 multiply_reduce_fusion.32
  252.0 2.0 multiply_reduce_fusion.32
  (563 shorter events, 121.4 us)
Async XLA Ops:
  0.6 7.6 %copy-start = (f32[8,2048]{1,0:T(8,128)S(1)}, f32[8,2048]{1,0:T(8,128)}, u32[]{:S(2)}) copy-start(f32[8,2048]{1,0:T(8,128)} %param.22) | copy-start | bytes 196612
  2.4 9.9 %all-to-all-start.1 = ((s32[8,4,1]{1,2,0:T(1,128)}), s32[8,4,1]{1,2,0:T(1,128)S(1)}, u32[]{:S(2)}, u32[]{:S(2)}) async-start(s32[8,4,1]{1,2,0:T(1,128)} %bitcast.89), calls=%async_computation.1 | async-start | bytes 8192 | tf_op jit(solution)/shard_map/all_to_all | solution.py:123
  12.3 9.2 %all-to-all-start = ((f32[32,8,128]{2,1,0:T(8,128)}), f32[32,8,128]{2,1,0:T(8,128)S(1)}, u32[]{:S(2)}, u32[]{:S(2)}) async-start(f32[32,8,128]{2,1,0:T(8,128)} %copy.49), calls=%async_computation | async-start | bytes 262144 | tf_op jit(solution)/shard_map/all_to_all | solution.py:122
  21.6 7.8 %collective-permute-start = (f32[6,4,128]{2,1,0:T(4,128)S(1)}, f32[6,4,128]{2,1,0:T(4,128)S(1)}, u32[]{:S(2)}, u32[]{:S(2)}) collective-permute-start(f32[6,4,128]{2,1,0:T(4,128)S(1)} %get-tuple-element.782), channel_id=1, source_target_pairs={{0,1},{1,2},{2,3},{3,4},{4,5},{5,6},{6,7},{7,8},{8,9},{9,10},{10,1... | collective-permute-start | bytes 36872 | tf_op jit(solution)/shard_map/ppermute | solution.py:20
  27.5 6.8 %collective-permute-start.1 = (f32[6,4,128]{2,1,0:T(4,128)S(1)}, f32[6,4,128]{2,1,0:T(4,128)S(1)}, u32[]{:S(2)}, u32[]{:S(2)}) collective-permute-start(f32[6,4,128]{2,1,0:T(4,128)S(1)} %get-tuple-element.783), channel_id=1, source_target_pairs={{1,0},{2,1},{3,2},{4,3},{5,4},{6,5},{7,6},{8,7},{9,8},{10,9},{11,1... | collective-permute-start | bytes 36872 | tf_op jit(solution)/shard_map/ppermute | solution.py:20
  49.7 4.4 %collective-permute-start.2 = (f32[1,4,128]{2,1,0:T(4,128)S(1)}, f32[1,4,128]{2,1,0:T(4,128)S(1)}, u32[]{:S(2)}, u32[]{:S(2)}) collective-permute-start(f32[1,4,128]{2,1,0:T(4,128)S(1)} %get-tuple-element.794), channel_id=1, source_target_pairs={{0,1},{1,2},{2,3},{3,4},{4,5},{5,6},{6,7},{7,8},{8,9},{9,10},{10,1... | collective-permute-start | bytes 6152 | tf_op jit(solution)/shard_map/ppermute | solution.py:20
  51.6 6.7 %collective-permute-start.3 = (f32[1,4,128]{2,1,0:T(4,128)S(1)}, f32[1,4,128]{2,1,0:T(4,128)S(1)}, u32[]{:S(2)}, u32[]{:S(2)}) collective-permute-start(f32[1,4,128]{2,1,0:T(4,128)S(1)} %get-tuple-element.795), channel_id=1, source_target_pairs={{1,0},{2,1},{3,2},{4,3},{5,4},{6,5},{7,6},{8,7},{9,8},{10,9},{11,1... | collective-permute-start | bytes 6152 | tf_op jit(solution)/shard_map/ppermute | solution.py:20
  83.0 4.3 %collective-permute-start.4 = (f32[1,4,128]{2,1,0:T(4,128)S(1)}, f32[1,4,128]{2,1,0:T(4,128)S(1)}, u32[]{:S(2)}, u32[]{:S(2)}) collective-permute-start(f32[1,4,128]{2,1,0:T(4,128)S(1)} %get-tuple-element.792), channel_id=1, source_target_pairs={{0,1},{1,2},{2,3},{3,4},{4,5},{5,6},{6,7},{7,8},{8,9},{9,10},{10,1... | collective-permute-start | bytes 6152 | tf_op jit(solution)/shard_map/ppermute | solution.py:20
  85.0 6.7 %collective-permute-start.5 = (f32[1,4,128]{2,1,0:T(4,128)S(1)}, f32[1,4,128]{2,1,0:T(4,128)S(1)}, u32[]{:S(2)}, u32[]{:S(2)}) collective-permute-start(f32[1,4,128]{2,1,0:T(4,128)S(1)} %get-tuple-element.793), channel_id=1, source_target_pairs={{1,0},{2,1},{3,2},{4,3},{5,4},{6,5},{7,6},{8,7},{9,8},{10,9},{11,1... | collective-permute-start | bytes 6152 | tf_op jit(solution)/shard_map/ppermute | solution.py:20
  117.8 4.5 %collective-permute-start.6 = (f32[1,4,128]{2,1,0:T(4,128)S(1)}, f32[1,4,128]{2,1,0:T(4,128)S(1)}, u32[]{:S(2)}, u32[]{:S(2)}) collective-permute-start(f32[1,4,128]{2,1,0:T(4,128)S(1)} %get-tuple-element.790), channel_id=1, source_target_pairs={{0,1},{1,2},{2,3},{3,4},{4,5},{5,6},{6,7},{7,8},{8,9},{9,10},{10,1... | collective-permute-start | bytes 6152 | tf_op jit(solution)/shard_map/ppermute | solution.py:20
  119.8 6.7 %collective-permute-start.7 = (f32[1,4,128]{2,1,0:T(4,128)S(1)}, f32[1,4,128]{2,1,0:T(4,128)S(1)}, u32[]{:S(2)}, u32[]{:S(2)}) collective-permute-start(f32[1,4,128]{2,1,0:T(4,128)S(1)} %get-tuple-element.791), channel_id=1, source_target_pairs={{1,0},{2,1},{3,2},{4,3},{5,4},{6,5},{7,6},{8,7},{9,8},{10,9},{11,1... | collective-permute-start | bytes 6152 | tf_op jit(solution)/shard_map/ppermute | solution.py:20
  151.1 4.3 %collective-permute-start.8 = (f32[1,4,128]{2,1,0:T(4,128)S(1)}, f32[1,4,128]{2,1,0:T(4,128)S(1)}, u32[]{:S(2)}, u32[]{:S(2)}) collective-permute-start(f32[1,4,128]{2,1,0:T(4,128)S(1)} %get-tuple-element.788), channel_id=1, source_target_pairs={{0,1},{1,2},{2,3},{3,4},{4,5},{5,6},{6,7},{7,8},{8,9},{9,10},{10,1... | collective-permute-start | bytes 6152 | tf_op jit(solution)/shard_map/ppermute | solution.py:20
  153.1 6.7 %collective-permute-start.9 = (f32[1,4,128]{2,1,0:T(4,128)S(1)}, f32[1,4,128]{2,1,0:T(4,128)S(1)}, u32[]{:S(2)}, u32[]{:S(2)}) collective-permute-start(f32[1,4,128]{2,1,0:T(4,128)S(1)} %get-tuple-element.789), channel_id=1, source_target_pairs={{1,0},{2,1},{3,2},{4,3},{5,4},{6,5},{7,6},{8,7},{9,8},{10,9},{11,1... | collective-permute-start | bytes 6152 | tf_op jit(solution)/shard_map/ppermute | solution.py:20
  185.9 4.3 %collective-permute-start.10 = (f32[1,4,128]{2,1,0:T(4,128)S(1)}, f32[1,4,128]{2,1,0:T(4,128)S(1)}, u32[]{:S(2)}, u32[]{:S(2)}) collective-permute-start(f32[1,4,128]{2,1,0:T(4,128)S(1)} %get-tuple-element.786), channel_id=1, source_target_pairs={{0,1},{1,2},{2,3},{3,4},{4,5},{5,6},{6,7},{7,8},{8,9},{9,10},{10,1... | collective-permute-start | bytes 6152 | tf_op jit(solution)/shard_map/ppermute | solution.py:20
  187.9 6.7 %collective-permute-start.11 = (f32[1,4,128]{2,1,0:T(4,128)S(1)}, f32[1,4,128]{2,1,0:T(4,128)S(1)}, u32[]{:S(2)}, u32[]{:S(2)}) collective-permute-start(f32[1,4,128]{2,1,0:T(4,128)S(1)} %get-tuple-element.787), channel_id=1, source_target_pairs={{1,0},{2,1},{3,2},{4,3},{5,4},{6,5},{7,6},{8,7},{9,8},{10,9},{11,1... | collective-permute-start | bytes 6152 | tf_op jit(solution)/shard_map/ppermute | solution.py:20
  219.3 4.6 %collective-permute-start.12 = (f32[1,4,128]{2,1,0:T(4,128)S(1)}, f32[1,4,128]{2,1,0:T(4,128)S(1)}, u32[]{:S(2)}, u32[]{:S(2)}) collective-permute-start(f32[1,4,128]{2,1,0:T(4,128)S(1)} %get-tuple-element.784), channel_id=1, source_target_pairs={{0,1},{1,2},{2,3},{3,4},{4,5},{5,6},{6,7},{7,8},{8,9},{9,10},{10,1... | collective-permute-start | bytes 6152 | tf_op jit(solution)/shard_map/ppermute | solution.py:20
  221.2 6.7 %collective-permute-start.13 = (f32[1,4,128]{2,1,0:T(4,128)S(1)}, f32[1,4,128]{2,1,0:T(4,128)S(1)}, u32[]{:S(2)}, u32[]{:S(2)}) collective-permute-start(f32[1,4,128]{2,1,0:T(4,128)S(1)} %get-tuple-element.785), channel_id=1, source_target_pairs={{1,0},{2,1},{3,2},{4,3},{5,4},{6,5},{7,6},{8,7},{9,8},{10,9},{11,1... | collective-permute-start | bytes 6152 | tf_op jit(solution)/shard_map/ppermute | solution.py:20
  254.1 0.6 copy-start.1
  254.1 0.6 copy-start.2
where the time goes:
time: 256 us; the launch traced here: 255 us
  other arithmetic  77.9 us (30%)
  local copies, waits for them, and re-layouts  73.1 us (29%)
  starting transfers between devices  44.3 us (17%)
  waiting for transfers between devices  36.5 us (14%)
  loops' own time  20.6 us (8%)
    gather x148, local copies, waits for them, and re-layouts, one_block(): jnp.take(values, near_rows, axis=1)  50.6 us
    ppermute x14, starting transfers between devices, shifted(): lax.ppermute(value, axis, [(source, source + steps) for source in range(f...  34.1 us
    ppermute x14, waiting for transfers between devices, shifted(): lax.ppermute(value, axis, [(source, source + steps) for source in range(f...  30.3 us
    reduce_sum x12, other arithmetic, jacobi_kernel(): inflow = jnp.sum(coupling * near_energy[0][:, :, None, :], axis=(1, 3))  24.3 us
    another operation x7, loops' own time, tile_blocks(): blocks = lax.map(one_block, jnp.arange(block_count, dtype=jnp.int32))  20.6 us
    mul x12, other arithmetic, limiter_kernel(): scaled = volume[:, :, None, :] * forces * change  17.4 us
    dynamic_slice x28, local copies, waits for them, and re-layouts, tile_blocks(): blocks = lax.map(one_block, jnp.arange(block_count, dtype=jnp.int32))  16.4 us
    reduce_sum x28, other arithmetic, geometry(): distance = jnp.sqrt(jnp.sum(offsets * offsets, axis=0))  15.4 us
  transfers between devices with their start and end apart: 16, of which 9 were waited for; matrix products, arithmetic and copies ran while one was open for 1% of the time, Pallas kernels for 0%

commit v1 on v0

v1 whole, which is shorter than its diff:
```python
import functools
import math

import jax
import jax.numpy as jnp
from jax import lax
from jax.experimental import pallas as pl
from jax.experimental.pallas import tpu as pltpu
from jax.sharding import PartitionSpec as P

TILE = 128
GMAX = 4
SWEEPS = 3
CHUNK = 32
KERNEL_NORM = 21.0 / (16.0 * math.pi)
FORCE_NORM = 5.0 * KERNEL_NORM * 32.0
TIME_STEP = 0.05
SHIFT_E = 2.25
SHIFT_X = 0.5
MESH = pl.DeviceIdType.MESH
F32 = jnp.float32
BF16 = jnp.bfloat16


def row(value, count=8):
    return jnp.broadcast_to(value, (count, TILE))


def split_rows(value):
    high = value.astype(BF16)
    low = (value - high.astype(F32)).astype(BF16)
    return jnp.concatenate([high, low], axis=0)


def kernel(
    groups, members, tc, nb, cap,
    part_ref, slot_ref, near_ref, ghost_ref, energy_ref, density_ref,
    send_buf, recv_buf, ext, cols, force, acc_ref, dens, vol, gv, en, diff, lim, jac, sums,
    a2a_send, a2a_recv, halo_send, halo_recv,
):
    my_group = lax.axis_index("group")
    my_member = lax.axis_index("member")
    me = my_group * members + my_member
    count = groups * members
    has_left = me > 0
    has_right = me < count - 1
    left = lax.rem(me + count - 1, count)
    right = lax.rem(me + 1, count)
    left_id = (left // members, lax.rem(left, members))
    right_id = (right // members, lax.rem(right, members))
    edge = GMAX
    total = tc + 2 * edge

    barrier = pltpu.get_barrier_semaphore()

    def greet(offset, carry):
        target = lax.rem(my_group + offset, groups)
        pl.semaphore_signal(barrier, inc=1, device_id=(target, my_member), device_id_type=MESH)
        return carry

    lax.fori_loop(1, groups, greet, 0)
    for device in (left_id, right_id):
        pl.semaphore_signal(barrier, inc=1, device_id=device, device_id_type=MESH)

    targets = [slot_ref[t] // (tc * members) for t in range(tc)]
    places = []
    for t in range(tc):
        order = jnp.int32(0)
        for u in range(t):
            order = order + jnp.where(targets[u] == targets[t], 1, 0)
        places.append(targets[t] * cap + order)
    labels = [lax.rem(slot_ref[t], tc) + 1 for t in range(tc)]
    place_rows = [jnp.full((8, TILE), p, jnp.int32) for p in places]
    label_rows = [jnp.full((8, TILE), p, jnp.int32).astype(F32) for p in labels]

    def pack(group, carry):
        for c in range(cap):
            bucket = group * cap + c
            tile = jnp.zeros((8, TILE), F32)
            label = jnp.zeros((8, TILE), F32)
            for t in range(tc):
                mask = place_rows[t] == bucket
                tile = jnp.where(mask, part_ref[:, t * TILE : (t + 1) * TILE], tile)
                label = jnp.where(mask, label_rows[t], label)
            send_buf[group, c] = tile
            send_buf[group, cap, c : c + 1, :] = label[0:1]
        return carry

    lax.fori_loop(0, groups, pack, 0)
    pl.semaphore_wait(barrier, groups + 1)

    def a2a_copy(offset):
        target = lax.rem(my_group + offset, groups)
        return pltpu.make_async_remote_copy(
            src_ref=send_buf.at[target],
            dst_ref=recv_buf.at[my_group],
            send_sem=a2a_send.at[offset],
            recv_sem=a2a_recv.at[offset],
            device_id=(target, my_member),
            device_id_type=MESH,
        )

    def a2a_start(offset, carry):
        a2a_copy(offset).start()
        return carry

    def a2a_wait(offset, carry):
        a2a_copy(offset).wait()
        return carry

    lax.fori_loop(1, groups, a2a_start, 0)
    recv_buf[my_group] = send_buf[my_group]
    lax.fori_loop(1, groups, a2a_wait, 0)

    def choose(group, tiles):
        tiles = list(tiles)
        for c in range(cap):
            tile = recv_buf[group, c]
            label = row(recv_buf[group, cap, c : c + 1, :])
            for k in range(tc):
                tiles[k] = jnp.where(label == float(k + 1), tile, tiles[k])
        return tuple(tiles)

    arranged = lax.fori_loop(
        0, groups, choose, tuple(jnp.zeros((8, TILE), F32) for _ in range(tc))
    )
    for k in range(tc):
        ext[edge + k] = arranged[k]

    def halo_copies(number, ref):
        to_left = pltpu.make_async_remote_copy(
            src_ref=ref.at[pl.ds(edge, edge)],
            dst_ref=ref.at[pl.ds(edge + tc, edge)],
            send_sem=halo_send.at[number, 0],
            recv_sem=halo_recv.at[number, 0],
            device_id=left_id,
            device_id_type=MESH,
        )
        to_right = pltpu.make_async_remote_copy(
            src_ref=ref.at[pl.ds(tc, edge)],
            dst_ref=ref.at[pl.ds(0, edge)],
            send_sem=halo_send.at[number, 1],
            recv_sem=halo_recv.at[number, 1],
            device_id=right_id,
            device_id_type=MESH,
        )
        return to_left, to_right

    def halo_start(number, ref):
        to_left, to_right = halo_copies(number, ref)
        pl.when(has_left)(to_left.start)
        pl.when(has_right)(to_right.start)

    def halo_wait(number, ref):
        to_left, to_right = halo_copies(number, ref)
        pl.when(has_right)(to_left.wait_recv)
        pl.when(has_left)(to_right.wait_recv)

    def halo_done(number, ref):
        to_left, to_right = halo_copies(number, ref)
        pl.when(has_left)(to_left.wait_send)
        pl.when(has_right)(to_right.wait_send)

    base = edge - ghost_ref[0, 0]

    def columns(j):
        turned = jnp.transpose(ext[j])
        for place, field in enumerate((0, 1, 2, 3, 4)):
            cols[j, place] = jnp.broadcast_to(turned[:, field : field + 1], (TILE, TILE))
        return None

    def columns_step(j, carry):
        columns(j)
        return carry

    def pair_block(s, slot, j, acc):
        own = ext[edge + s]
        xi, yi, zi, hi = (own[f : f + 1] for f in (0, 1, 2, 4))
        xi, yi, zi, hi, ih = (row(v) for v in (xi, yi, zi, hi, 0.5 / hi))
        for first in range(0, TILE, CHUNK):
            span = pl.ds(first, CHUNK)
            big = (CHUNK // 8, 8, TILE)
            xb, yb, zb, mb, hb = (cols[j, f, span, :].reshape(big) for f in range(5))
            dx, dy, dz = xb - xi, yb - yi, zb - zi
            square = dx * dx + dy * dy + dz * dz
            r = square * lax.rsqrt(jnp.maximum(square, 1e-30))
            u = hb + hi
            inverse = 1.0 / (u * u)
            a = jnp.maximum(u - r, 0.0) * inverse
            f = (a * a) * (a * inverse)
            f = f.reshape(CHUNK, TILE)
            high = f.astype(BF16)
            low = (f - high.astype(F32)).astype(BF16)
            force[s * nb + slot, span, 0:TILE] = high
            force[s * nb + slot, span, TILE : 2 * TILE] = low
            t = jnp.maximum(1.0 - r * ih, 0.0)
            t2 = t * t
            w = (mb * (5.0 - 4.0 * t)) * (t2 * t2)
            acc = acc + jnp.sum(w, axis=0)
        return acc

    halo_start(0, ext)
    lax.fori_loop(edge, edge + tc, columns_step, 0)

    def self_step(s, carry):
        acc_ref[s] = pair_block(s, 0, edge + s, jnp.zeros((8, TILE), F32))
        return carry

    lax.fori_loop(0, tc, self_step, 0)
    halo_wait(0, ext)
    lax.fori_loop(0, edge, columns_step, 0)
    lax.fori_loop(edge + tc, total, columns_step, 0)

    def density_tile(s):
        def other(n, acc):
            return pair_block(s, n, near_ref[s, n] + base, acc)

        acc = lax.fori_loop(1, nb, other, acc_ref[s])
        h = ext[edge + s, 4:5, :]
        value = jnp.sum(acc, axis=0, keepdims=True) * (KERNEL_NORM / (h * h * h))
        dens[edge + s] = value
        density_ref[pl.ds(s, 1), :] = value

    def edge_tile(q):
        return q + (tc - 2 * edge) * (q // edge)

    def density_edge(q, carry):
        density_tile(edge_tile(q))
        return carry

    def density_mid(q, carry):
        density_tile(q)
        return carry

    lax.fori_loop(0, 2 * edge, density_edge, 0)
    halo_start(1, dens)
    lax.fori_loop(edge, tc - edge, density_mid, 0)

    rows = lax.broadcasted_iota(jnp.int32, (8, TILE), 0)
    top = rows < 4

    def limiter_rows(sweep, j):
        lim[j] = split_rows(gv[j] * jnp.where(top, row(en[sweep, j]), 1.0))

    def start_tile(j):
        own = ext[j]
        one_x = jnp.where(lax.rem(rows, 4) == 0, 1.0, pltpu.roll(own, 1, 0) - SHIFT_X)
        two = jnp.where(top, one_x, pltpu.roll(one_x, 4, 0))
        volume = FORCE_NORM * own[3:4] / dens[j]
        vol[j] = volume
        gv[j] = two * row(volume)
        en[0, j] = own[5:6] - SHIFT_E
        limiter_rows(0, j)

    def jacobi_rows(sweep, j):
        vd = row(vol[j] * diff[sweep, j])
        pick = jnp.where(rows == 0, row(en[sweep, j]), jnp.where(rows == 1, 1.0, 0.0))
        jac[j] = split_rows(vd * pick)

    def start_step(j, carry):
        start_tile(j)
        return carry

    def product(table, s):
        parts = [table[edge + s]] + [table[near_ref[s, n] + base] for n in range(1, nb)]
        left_side = jnp.concatenate(parts, axis=1)
        right_side = force[pl.ds(s * nb, nb)].reshape(nb * TILE, 2 * TILE)
        out = jnp.dot(left_side, right_side, preferred_element_type=F32)
        return (out[0:8, 0:TILE] + out[0:8, TILE:]) + (out[8:16, 0:TILE] + out[8:16, TILE:])

    def limiter_tile(sweep, s):
        value = product(lim, s)
        sums[s] = value
        e = en[sweep, edge + s]
        own = ext[edge + s]
        lead = value[0:1] - e * value[4:5]
        square = jnp.zeros((1, TILE), F32)
        for axis in range(3):
            g = value[1 + axis : 2 + axis] - e * value[5 + axis : 6 + axis]
            g = g - (own[axis : axis + 1] - SHIFT_X) * lead
            square = square + g * g
        opaque = own[6:7] * dens[edge + s]
        ratio = jnp.sqrt(square) / (opaque * (e + SHIFT_E))
        diff[sweep, edge + s] = (2.0 + ratio) / ((6.0 + 3.0 * ratio + ratio * ratio) * opaque)
        jacobi_rows(sweep, edge + s)

    def jacobi_tile(sweep, s):
        value = product(jac, s)
        own = ext[edge + s]
        old = sums[s]
        d = diff[sweep, edge + s]
        scale = TIME_STEP / dens[edge + s]
        inflow = d * old[0:1] + value[0:1]
        rate = d * old[4:5] + value[1:2]
        e = (own[5:6] - SHIFT_E + TIME_STEP * own[7:8] + scale * inflow) / (1.0 + scale * rate)
        if sweep == SWEEPS - 1:
            energy_ref[pl.ds(s, 1), :] = e + SHIFT_E
        else:
            en[sweep + 1, edge + s] = e
            limiter_rows(sweep + 1, edge + s)

    def four(work, first):
        for k in range(edge):
            work(first + k)

    def edges(work):
        lax.fori_loop(0, 2, lambda q, c: (four(work, q * (tc - edge)), c)[1], 0)

    def middle(work):
        lax.fori_loop(1, tc // edge - 1, lambda q, c: (four(work, q * edge), c)[1], 0)

    def ghosts(work):
        for j in range(edge):
            work(j)
            work(edge + tc + j)

    lax.fori_loop(edge, edge + tc, start_step, 0)
    halo_wait(1, dens)
    ghosts(start_tile)

    for sweep in range(SWEEPS):
        if sweep > 0:
            halo_wait(2 * sweep + 1, en.at[sweep])
            ghosts(functools.partial(limiter_rows, sweep))
        work = functools.partial(limiter_tile, sweep)
        edges(work)
        halo_start(2 * sweep + 2, diff.at[sweep])
        middle(work)
        halo_wait(2 * sweep + 2, diff.at[sweep])
        ghosts(functools.partial(jacobi_rows, sweep))
        work = functools.partial(jacobi_tile, sweep)
        edges(work)
        if sweep < SWEEPS - 1:
            halo_start(2 * sweep + 3, en.at[sweep + 1])
        middle(work)

    halo_done(0, ext)
    halo_done(1, dens)
    for sweep in range(SWEEPS):
        halo_done(2 * sweep + 2, diff.at[sweep])
        if sweep < SWEEPS - 1:
            halo_done(2 * sweep + 3, en.at[sweep + 1])


def solution(mesh):
    groups, members = mesh.shape["group"], mesh.shape["member"]

    def local(particles, new_slot, neighbours, ghosts):
        tc = new_slot.shape[0]
        nb = neighbours.shape[1]
        cap = max(2, (2 * tc + groups - 1) // groups)
        total = tc + 2 * GMAX
        halos = 2 + 2 * SWEEPS - 1
        vmem = pl.BlockSpec(memory_space=pltpu.VMEM)
        smem = pl.BlockSpec(memory_space=pltpu.SMEM)
        energy, density = pl.pallas_call(
            functools.partial(kernel, groups, members, tc, nb, cap),
            out_shape=[jax.ShapeDtypeStruct((tc, TILE), F32)] * 2,
            in_specs=[vmem, smem, smem, smem],
            out_specs=[vmem, vmem],
            scratch_shapes=[
                pltpu.VMEM((groups, cap + 1, 8, TILE), F32),
                pltpu.VMEM((groups, cap + 1, 8, TILE), F32),
                pltpu.VMEM((total, 8, TILE), F32),
                pltpu.VMEM((total, 5, TILE, TILE), F32),
                pltpu.VMEM((tc * nb, TILE, 2 * TILE), BF16),
                pltpu.VMEM((tc, 8, TILE), F32),
                pltpu.VMEM((total, 1, TILE), F32),
                pltpu.VMEM((total, 1, TILE), F32),
                pltpu.VMEM((total, 8, TILE), F32),
                pltpu.VMEM((SWEEPS, total, 1, TILE), F32),
                pltpu.VMEM((SWEEPS, total, 1, TILE), F32),
                pltpu.VMEM((total, 16, TILE), BF16),
                pltpu.VMEM((total, 16, TILE), BF16),
                pltpu.VMEM((tc, 8, TILE), F32),
                pltpu.SemaphoreType.DMA((groups,)),
                pltpu.SemaphoreType.DMA((groups,)),
                pltpu.SemaphoreType.DMA((halos, 2)),
                pltpu.SemaphoreType.DMA((halos, 2)),
            ],
            compiler_params=pltpu.CompilerParams(
                collective_id=0, has_side_effects=True, vmem_limit_bytes=60 * 1024 * 1024
            ),
        )(particles, new_slot, neighbours, ghosts)
        return energy.reshape(-1), density.reshape(-1)

    in_specs = (
        P(None, ("group", "member")),
        P(("group", "member")),
        P(("group", "member"), None),
        P(("group", "member"), None),
    )
    out_specs = (P(("group", "member")), P(("group", "member")))
    return jax.shard_map(local, mesh=mesh, in_specs=in_specs, out_specs=out_specs, check_vma=False)
```

time: 256 us -> 50.6 us (0.20)
  other arithmetic: 77.9 us -> 0 us
  local copies, waits for them, and re-layouts: 73.1 us -> 3.27 us
  Pallas kernels: 0 us -> 46.5 us
  starting transfers between devices: 44.3 us -> 0 us
  waiting for transfers between devices: 36.5 us -> 0 us
  loops' own time: 20.6 us -> 0 us
    reduce_sum x70 -> x0, other arithmetic: 54.1 us -> none  [the longest x12 24.3 us: jacobi_kernel(): inflow = jnp.sum(coupling * near_energy[0][:, :, None, :], axis=(1, 3))]
    gather x148 -> x0, local copies, waits for them, and re-layouts: 50.6 us -> none  [one_block(): jnp.take(values, near_rows, axis=1)]
    pallas_call x0 -> x1, Pallas kernels: none -> 46.5 us  [local(): pl.pallas_call(functools.partial(kernel, groups, members, tc, nb, cap), o...]
    ppermute x14 -> x0, starting transfers between devices: 34.1 us -> none  [shifted(): lax.ppermute(value, axis, [(source, source + steps) for source in range(f...]
    ppermute x14 -> x0, waiting for transfers between devices: 30.3 us -> none  [shifted(): lax.ppermute(value, axis, [(source, source + steps) for source in range(f...]
    another operation x7 -> x0, loops' own time: 20.6 us -> none  [tile_blocks(): blocks = lax.map(one_block, jnp.arange(block_count, dtype=jnp.int32))]
    mul x24 -> x0, other arithmetic: 18.3 us -> none  [the longest x12 17.4 us: limiter_kernel(): scaled = volume[:, :, None, :] * forces * change]
    dynamic_slice x28 -> x0, local copies, waits for them, and re-layouts: 16.4 us -> none  [tile_blocks(): blocks = lax.map(one_block, jnp.arange(block_count, dtype=jnp.int32))]
  transfers between devices with their start and end apart: 16 -> 0, of which waited for: 9 -> 0; matrix products, arithmetic and copies ran while one was open for 1% -> 0% of each run, Pallas kernels for 0% -> 0%
where the time goes in v1:
time: 50.6 us; the launch traced here: 50.4 us
  Pallas kernels  46.5 us (92%)
  local copies, waits for them, and re-layouts  3.27 us (6%)
  between operations  0.65 us (1%)
    pallas_call x1, Pallas kernels, local(): pl.pallas_call(functools.partial(kernel, groups, members, tc, nb, cap), o...  46.5 us
    unnamed x5, local copies, waits for them, and re-layouts  3.27 us

profile of v1, /device:TPU:7, one launch (start us, length us, event | category | flops | bytes accessed | tf_op | source)
XLA Modules:
  0.0 50.4 jit_solution(13572308927650141357)
XLA Ops:
  0.6 1.4 %copy.6.near_ref = s32[16,6]{1,0:T(8,128)} copy(s32[16,6]{0,1:T(8,128)} %param.6) | data formatting | bytes 768 | tf_op args[2]
  2.0 46.5 %shard_map.59 = (f32[16,128]{1,0:T(8,128)}, f32[16,128]{1,0:T(8,128)}) custom-call(f32[8,2048]{1,0:T(8,128)} %part_ref.1, s32[16]{0:T(128)} %slot_ref.1, s32[16,6]{1,0:T(8,128)} %copy.6.near_ref, s32[1,2]{1,0:T(1,128)} %ghost_ref.1), custom_call_target="tpu_custom_call" | custom-call | tf_op jit(solution)/shard_map/pallas_call | solution.py:356
  48.5 0.0 copy-start
  48.5 1.3 %copy.9 = f32[2048]{0:T(1024)} copy(f32[2048]{0:T(1024)} %bitcast.3) | data formatting | bytes 16384
  49.8 0.0 copy-done
  49.8 0.6 %copy.10 = f32[2048]{0:T(1024)} copy(f32[2048]{0:T(1024)S(1)} %bitcast.2) | data formatting | bytes 16384
Async XLA Ops:
  48.5 1.3 %copy-start = (f32[16,128]{1,0:T(8,128)S(1)}, f32[16,128]{1,0:T(8,128)}, u32[]{:S(2)}) copy-start(f32[16,128]{1,0:T(8,128)} %get-tuple-element.5) | copy-start | bytes 24580

commit v2 on v1

--- a/solution.py
+++ b/solution.py
@@ -163,20 +163,35 @@
 
     base = edge - ghost_ref[0, 0]
 
+    part_row = lax.broadcasted_iota(jnp.int32, (32, 5 * TILE), 0)
+    part_col = lax.broadcasted_iota(jnp.int32, (32, 5 * TILE), 1)
+    spread = (
+        jnp.where(part_row < 24, 1.0, 0.0)
+        * jnp.where(lax.rem(part_row, 8) == part_col // TILE, 1.0, 0.0)
+    ).astype(BF16)
+
     def columns(j):
-        turned = jnp.transpose(ext[j])
-        for place, field in enumerate((0, 1, 2, 3, 4)):
-            cols[j, place] = jnp.broadcast_to(turned[:, field : field + 1], (TILE, TILE))
-        return None
-
-    def columns_step(j, carry):
-        columns(j)
+        fields = ext[j]
+        first = fields.astype(BF16).astype(F32)
+        rest = fields - first
+        second = rest.astype(BF16).astype(F32)
+        third = rest - second
+        stacked = jnp.concatenate([first, second, third, jnp.zeros((8, TILE), F32)], axis=0)
+        turned = jnp.transpose(stacked).astype(BF16)
+        wide = jnp.dot(turned, spread, preferred_element_type=F32)
+        for place in range(5):
+            cols[j, place] = wide[:, place * TILE : (place + 1) * TILE]
+
+    def columns_step(q, carry):
+        for k in range(edge):
+            columns(q * edge + k)
         return carry
 
     def pair_block(s, slot, j, acc):
         own = ext[edge + s]
         xi, yi, zi, hi = (own[f : f + 1] for f in (0, 1, 2, 4))
-        xi, yi, zi, hi, ih = (row(v) for v in (xi, yi, zi, hi, 0.5 / hi))
+        reach, half = row(2.0 * hi), row(0.5 * hi)
+        xi, yi, zi, hi = (row(v) for v in (xi, yi, zi, hi))
         for first in range(0, TILE, CHUNK):
             span = pl.ds(first, CHUNK)
             big = (CHUNK // 8, 8, TILE)
@@ -191,16 +206,16 @@
             f = f.reshape(CHUNK, TILE)
             high = f.astype(BF16)
             low = (f - high.astype(F32)).astype(BF16)
-            force[s * nb + slot, span, 0:TILE] = high
-            force[s * nb + slot, span, TILE : 2 * TILE] = low
-            t = jnp.maximum(1.0 - r * ih, 0.0)
+            force[0, s * nb + slot, span, :] = high
+            force[1, s * nb + slot, span, :] = low
+            t = jnp.maximum(reach - r, 0.0)
             t2 = t * t
-            w = (mb * (5.0 - 4.0 * t)) * (t2 * t2)
+            w = (mb * (half + r)) * (t2 * t2)
             acc = acc + jnp.sum(w, axis=0)
         return acc
 
     halo_start(0, ext)
-    lax.fori_loop(edge, edge + tc, columns_step, 0)
+    lax.fori_loop(1, 1 + tc // edge, columns_step, 0)
 
     def self_step(s, carry):
         acc_ref[s] = pair_block(s, 0, edge + s, jnp.zeros((8, TILE), F32))
@@ -208,16 +223,18 @@
 
     lax.fori_loop(0, tc, self_step, 0)
     halo_wait(0, ext)
-    lax.fori_loop(0, edge, columns_step, 0)
-    lax.fori_loop(edge + tc, total, columns_step, 0)
+    columns_step(0, 0)
+    columns_step(1 + tc // edge, 0)
 
     def density_tile(s):
         def other(n, acc):
-            return pair_block(s, n, near_ref[s, n] + base, acc)
+            return pair_block(s, n, near_ref[n, s] + base, acc)
 
         acc = lax.fori_loop(1, nb, other, acc_ref[s])
         h = ext[edge + s, 4:5, :]
-        value = jnp.sum(acc, axis=0, keepdims=True) * (KERNEL_NORM / (h * h * h))
+        h2 = h * h
+        h4 = h2 * h2
+        value = jnp.sum(acc, axis=0, keepdims=True) * ((KERNEL_NORM / 8.0) / (h4 * h4))
         dens[edge + s] = value
         density_ref[pl.ds(s, 1), :] = value
 
@@ -262,9 +279,11 @@
         return carry
 
     def product(table, s):
-        parts = [table[edge + s]] + [table[near_ref[s, n] + base] for n in range(1, nb)]
+        parts = [table[edge + s]] + [table[near_ref[n, s] + base] for n in range(1, nb)]
         left_side = jnp.concatenate(parts, axis=1)
-        right_side = force[pl.ds(s * nb, nb)].reshape(nb * TILE, 2 * TILE)
+        right_side = jnp.concatenate(
+            [force[k, pl.ds(s * nb, nb)].reshape(nb * TILE, TILE) for k in range(2)], axis=1
+        )
         out = jnp.dot(left_side, right_side, preferred_element_type=F32)
         return (out[0:8, 0:TILE] + out[0:8, TILE:]) + (out[8:16, 0:TILE] + out[8:16, TILE:])
 
@@ -363,7 +382,7 @@
                 pltpu.VMEM((groups, cap + 1, 8, TILE), F32),
                 pltpu.VMEM((total, 8, TILE), F32),
                 pltpu.VMEM((total, 5, TILE, TILE), F32),
-                pltpu.VMEM((tc * nb, TILE, 2 * TILE), BF16),
+                pltpu.VMEM((2, tc * nb, TILE, TILE), BF16),
                 pltpu.VMEM((tc, 8, TILE), F32),
                 pltpu.VMEM((total, 1, TILE), F32),
                 pltpu.VMEM((total, 1, TILE), F32),
@@ -381,7 +400,7 @@
             compiler_params=pltpu.CompilerParams(
                 collective_id=0, has_side_effects=True, vmem_limit_bytes=60 * 1024 * 1024
             ),
-        )(particles, new_slot, neighbours, ghosts)
+        )(particles, new_slot, neighbours.T, ghosts)
         return energy.reshape(-1), density.reshape(-1)
 
     in_specs = (

time: 50.6 us -> 44.5 us (0.88)
  Pallas kernels: 46.5 us -> 41.3 us
  local copies, waits for them, and re-layouts: 3.27 us -> 1.9 us
    pallas_call x1, Pallas kernels: 46.5 us -> 41.3 us  [local(): pl.pallas_call(functools.partial(kernel, groups, members, tc, nb, cap), o...]
    unnamed x5 -> x4, local copies, waits for them, and re-layouts: 3.27 us -> 1.9 us
where the time goes in v2:
time: 44.5 us; the launch traced here: 43.9 us
  Pallas kernels  41.3 us (93%)
  local copies, waits for them, and re-layouts  1.9 us (4%)
  between operations  0.65 us (1%)
    pallas_call x1, Pallas kernels, local(): pl.pallas_call(functools.partial(kernel, groups, members, tc, nb, cap), o...  41.3 us
    unnamed x4, local copies, waits for them, and re-layouts  1.9 us

profile of v2, /device:TPU:7, one launch (start us, length us, event | category | flops | bytes accessed | tf_op | source)
XLA Modules:
  0.0 43.9 jit_solution(7771671757067142840)
XLA Ops:
  0.6 41.3 %shard_map.59 = (f32[16,128]{1,0:T(8,128)}, f32[16,128]{1,0:T(8,128)}) custom-call(f32[8,2048]{1,0:T(8,128)} %part_ref.1, s32[16]{0:T(128)} %slot_ref.1, s32[6,16]{1,0:T(8,128)} %bitcast.5, s32[1,2]{1,0:T(1,128)} %ghost_ref.1), custom_call_target="tpu_custom_call" | custom-call | tf_op jit(solution)/shard_map/pallas_call | solution.py:375
  42.0 0.0 copy-start
  42.0 1.3 %copy.8 = f32[2048]{0:T(1024)} copy(f32[2048]{0:T(1024)} %bitcast.4) | data formatting | bytes 16384
  43.3 0.0 copy-done
  43.3 0.6 %copy.9 = f32[2048]{0:T(1024)} copy(f32[2048]{0:T(1024)S(1)} %bitcast.3) | data formatting | bytes 16384
Async XLA Ops:
  42.0 1.3 %copy-start = (f32[16,128]{1,0:T(8,128)S(1)}, f32[16,128]{1,0:T(8,128)}, u32[]{:S(2)}) copy-start(f32[16,128]{1,0:T(8,128)} %get-tuple-element.5) | copy-start | bytes 24580

commit v3 on v2

--- a/solution.py
+++ b/solution.py
@@ -227,10 +227,9 @@
     columns_step(1 + tc // edge, 0)
 
     def density_tile(s):
-        def other(n, acc):
-            return pair_block(s, n, near_ref[n, s] + base, acc)
-
-        acc = lax.fori_loop(1, nb, other, acc_ref[s])
+        acc = acc_ref[s]
+        for n in range(1, nb):
+            acc = pair_block(s, n, near_ref[n, s] + base, acc)
         h = ext[edge + s, 4:5, :]
         h2 = h * h
         h4 = h2 * h2
@@ -318,15 +317,14 @@
             en[sweep + 1, edge + s] = e
             limiter_rows(sweep + 1, edge + s)
 
-    def four(work, first):
+    def edges(work):
         for k in range(edge):
-            work(first + k)
-
-    def edges(work):
-        lax.fori_loop(0, 2, lambda q, c: (four(work, q * (tc - edge)), c)[1], 0)
+            work(k)
+            work(tc - edge + k)
 
     def middle(work):
-        lax.fori_loop(1, tc // edge - 1, lambda q, c: (four(work, q * edge), c)[1], 0)
+        for s in range(edge, tc - edge):
+            work(s)
 
     def ghosts(work):
         for j in range(edge):

time: 44.5 us -> 42.1 us (0.946)
  Pallas kernels: 41.3 us -> 39.2 us
    pallas_call x1, Pallas kernels: 41.3 us -> 39.2 us  [local(): pl.pallas_call(functools.partial(kernel, groups, members, tc, nb, cap), o...]
where the time goes in v3:
time: 42.1 us; the launch traced here: 41.8 us
  Pallas kernels  39.2 us (93%)
  local copies, waits for them, and re-layouts  1.9 us (5%)
  between operations  0.65 us (2%)
    pallas_call x1, Pallas kernels, local(): pl.pallas_call(functools.partial(kernel, groups, members, tc, nb, cap), o...  39.2 us
    unnamed x4, local copies, waits for them, and re-layouts  1.9 us

profile of v3, /device:TPU:7, one launch (start us, length us, event | category | flops | bytes accessed | tf_op | source)
XLA Modules:
  0.0 41.8 jit_solution(6506069370487292187)
XLA Ops:
  0.6 39.2 %shard_map.59 = (f32[16,128]{1,0:T(8,128)}, f32[16,128]{1,0:T(8,128)}) custom-call(f32[8,2048]{1,0:T(8,128)} %part_ref.1, s32[16]{0:T(128)} %slot_ref.1, s32[6,16]{1,0:T(8,128)} %bitcast.5, s32[1,2]{1,0:T(1,128)} %ghost_ref.1), custom_call_target="tpu_custom_call" | custom-call | tf_op jit(solution)/shard_map/pallas_call | solution.py:373
  39.9 0.0 copy-start
  39.9 1.3 %copy.8 = f32[2048]{0:T(1024)} copy(f32[2048]{0:T(1024)} %bitcast.4) | data formatting | bytes 16384
  41.2 0.0 copy-done
  41.2 0.6 %copy.9 = f32[2048]{0:T(1024)} copy(f32[2048]{0:T(1024)S(1)} %bitcast.3) | data formatting | bytes 16384
Async XLA Ops:
  39.9 1.3 %copy-start = (f32[16,128]{1,0:T(8,128)S(1)}, f32[16,128]{1,0:T(8,128)}, u32[]{:S(2)}) copy-start(f32[16,128]{1,0:T(8,128)} %get-tuple-element.5) | copy-start | bytes 24580

commit v4 on v3

--- a/solution.py
+++ b/solution.py
@@ -35,7 +35,7 @@
 def kernel(
     groups, members, tc, nb, cap,
     part_ref, slot_ref, near_ref, ghost_ref, energy_ref, density_ref,
-    send_buf, recv_buf, ext, cols, force, acc_ref, dens, vol, gv, en, diff, lim, jac, sums,
+    send_buf, recv_buf, ext, cols, force, acc_ref, dens, vol, gv, en, diff, lim, jac, sums, dist,
     a2a_send, a2a_recv, halo_send, halo_recv,
 ):
     my_group = lax.axis_index("group")
@@ -187,7 +187,24 @@
             columns(q * edge + k)
         return carry
 
-    def pair_block(s, slot, j, acc):
+    def store_force(s, slot, span, r, u):
+        inverse = 1.0 / (u * u)
+        a = jnp.maximum(u - r, 0.0) * inverse
+        f = (a * a) * (a * inverse)
+        f = f.reshape(CHUNK, TILE)
+        high = f.astype(BF16)
+        force[0, s * nb + slot, span, :] = high
+        force[1, s * nb + slot, span, :] = (f - high.astype(F32)).astype(BF16)
+
+    def force_block(s, slot, j):
+        hi = row(ext[edge + s][4:5])
+        for first in range(0, TILE, CHUNK):
+            span = pl.ds(first, CHUNK)
+            big = (CHUNK // 8, 8, TILE)
+            r = dist[(s - edge) * nb + slot, span, :].reshape(big)
+            store_force(s, slot, span, r, cols[j, 4, span, :].reshape(big) + hi)
+
+    def pair_block(s, slot, j, acc, keep=False):
         own = ext[edge + s]
         xi, yi, zi, hi = (own[f : f + 1] for f in (0, 1, 2, 4))
         reach, half = row(2.0 * hi), row(0.5 * hi)
@@ -199,15 +216,10 @@
             dx, dy, dz = xb - xi, yb - yi, zb - zi
             square = dx * dx + dy * dy + dz * dz
             r = square * lax.rsqrt(jnp.maximum(square, 1e-30))
-            u = hb + hi
-            inverse = 1.0 / (u * u)
-            a = jnp.maximum(u - r, 0.0) * inverse
-            f = (a * a) * (a * inverse)
-            f = f.reshape(CHUNK, TILE)
-            high = f.astype(BF16)
-            low = (f - high.astype(F32)).astype(BF16)
-            force[0, s * nb + slot, span, :] = high
-            force[1, s * nb + slot, span, :] = low
+            if keep:
+                dist[(s - edge) * nb + slot, span, :] = r.reshape(CHUNK, TILE)
+            else:
+                store_force(s, slot, span, r, hb + hi)
             t = jnp.maximum(reach - r, 0.0)
             t2 = t * t
             w = (mb * (half + r)) * (t2 * t2)
@@ -226,10 +238,10 @@
     columns_step(0, 0)
     columns_step(1 + tc // edge, 0)
 
-    def density_tile(s):
+    def density_tile(s, keep):
         acc = acc_ref[s]
         for n in range(1, nb):
-            acc = pair_block(s, n, near_ref[n, s] + base, acc)
+            acc = pair_block(s, n, near_ref[n, s] + base, acc, keep)
         h = ext[edge + s, 4:5, :]
         h2 = h * h
         h4 = h2 * h2
@@ -241,11 +253,16 @@
         return q + (tc - 2 * edge) * (q // edge)
 
     def density_edge(q, carry):
-        density_tile(edge_tile(q))
+        density_tile(edge_tile(q), False)
         return carry
 
     def density_mid(q, carry):
-        density_tile(q)
+        density_tile(q, True)
+        return carry
+
+    def force_mid(s, carry):
+        for n in range(1, nb):
+            force_block(s, n, near_ref[n, s] + base)
         return carry
 
     lax.fori_loop(0, 2 * edge, density_edge, 0)
@@ -317,10 +334,21 @@
             en[sweep + 1, edge + s] = e
             limiter_rows(sweep + 1, edge + s)
 
-    def edges(work):
+    flag = my_member // max(members - 1, 1)
+
+    def edges(work, number=None, ref=None):
+        lead = (tc - edge) * flag
         for k in range(edge):
-            work(k)
-            work(tc - edge + k)
+            work(lead + k)
+        if ref is not None:
+            to_left, to_right = halo_copies(number, ref)
+            pl.when(jnp.logical_and(has_left, flag == 0))(to_left.start)
+            pl.when(jnp.logical_and(has_right, flag > 0))(to_right.start)
+        for k in range(edge):
+            work(tc - edge - lead + k)
+        if ref is not None:
+            pl.when(jnp.logical_and(has_right, flag == 0))(to_right.start)
+            pl.when(jnp.logical_and(has_left, flag > 0))(to_left.start)
 
     def middle(work):
         for s in range(edge, tc - edge):
@@ -340,15 +368,17 @@
             halo_wait(2 * sweep + 1, en.at[sweep])
             ghosts(functools.partial(limiter_rows, sweep))
         work = functools.partial(limiter_tile, sweep)
-        edges(work)
-        halo_start(2 * sweep + 2, diff.at[sweep])
+        edges(work, 2 * sweep + 2, diff.at[sweep])
+        if sweep == 0:
+            lax.fori_loop(edge, tc - edge, force_mid, 0)
         middle(work)
         halo_wait(2 * sweep + 2, diff.at[sweep])
         ghosts(functools.partial(jacobi_rows, sweep))
         work = functools.partial(jacobi_tile, sweep)
-        edges(work)
         if sweep < SWEEPS - 1:
-            halo_start(2 * sweep + 3, en.at[sweep + 1])
+            edges(work, 2 * sweep + 3, en.at[sweep + 1])
+        else:
+            edges(work)
         middle(work)
 
     halo_done(0, ext)
@@ -390,6 +420,7 @@
                 pltpu.VMEM((total, 16, TILE), BF16),
                 pltpu.VMEM((total, 16, TILE), BF16),
                 pltpu.VMEM((tc, 8, TILE), F32),
+                pltpu.VMEM(((tc - 2 * GMAX) * nb, TILE, TILE), F32),
                 pltpu.SemaphoreType.DMA((groups,)),
                 pltpu.SemaphoreType.DMA((groups,)),
                 pltpu.SemaphoreType.DMA((halos, 2)),

time: 42.1 us -> 40.9 us (0.971)
  Pallas kernels: 39.2 us -> 38.2 us
    pallas_call x1, Pallas kernels: 39.2 us -> 38.2 us  [local(): pl.pallas_call(functools.partial(kernel, groups, members, tc, nb, cap), o...]
where the time goes in v4:
time: 40.9 us; the launch traced here: 40.7 us
  Pallas kernels  38.2 us (93%)
  local copies, waits for them, and re-layouts  1.9 us (5%)
  between operations  0.65 us (2%)
    pallas_call x1, Pallas kernels, local(): pl.pallas_call(functools.partial(kernel, groups, members, tc, nb, cap), o...  38.2 us
    unnamed x4, local copies, waits for them, and re-layouts  1.9 us

profile of v4, /device:TPU:7, one launch (start us, length us, event | category | flops | bytes accessed | tf_op | source)
XLA Modules:
  0.0 40.7 jit_solution(8751194904813526615)
XLA Ops:
  0.6 38.2 %shard_map.59 = (f32[16,128]{1,0:T(8,128)}, f32[16,128]{1,0:T(8,128)}) custom-call(f32[8,2048]{1,0:T(8,128)} %part_ref.1, s32[16]{0:T(128)} %slot_ref.1, s32[6,16]{1,0:T(8,128)} %bitcast.5, s32[1,2]{1,0:T(1,128)} %ghost_ref.1), custom_call_target="tpu_custom_call" | custom-call | tf_op jit(solution)/shard_map/pallas_call | solution.py:403
  38.8 0.0 copy-start
  38.8 1.3 %copy.8 = f32[2048]{0:T(1024)} copy(f32[2048]{0:T(1024)} %bitcast.4) | data formatting | bytes 16384
  40.1 0.0 copy-done
  40.1 0.6 %copy.9 = f32[2048]{0:T(1024)} copy(f32[2048]{0:T(1024)S(1)} %bitcast.3) | data formatting | bytes 16384
Async XLA Ops:
  38.8 1.3 %copy-start = (f32[16,128]{1,0:T(8,128)S(1)}, f32[16,128]{1,0:T(8,128)}, u32[]{:S(2)}) copy-start(f32[16,128]{1,0:T(8,128)} %get-tuple-element.5) | copy-start | bytes 24580

commit v5 on v4

--- a/solution.py
+++ b/solution.py
@@ -34,7 +34,7 @@
 
 def kernel(
     groups, members, tc, nb, cap,
-    part_ref, slot_ref, near_ref, ghost_ref, energy_ref, density_ref,
+    part_ref, slot_ref, near_ref, ghost_ref, out_ref,
     send_buf, recv_buf, ext, cols, force, acc_ref, dens, vol, gv, en, diff, lim, jac, sums, dist,
     a2a_send, a2a_recv, halo_send, halo_recv,
 ):
@@ -247,7 +247,7 @@
         h4 = h2 * h2
         value = jnp.sum(acc, axis=0, keepdims=True) * ((KERNEL_NORM / 8.0) / (h4 * h4))
         dens[edge + s] = value
-        density_ref[pl.ds(s, 1), :] = value
+        out_ref[1, pl.ds(s, 1), :] = value
 
     def edge_tile(q):
         return q + (tc - 2 * edge) * (q // edge)
@@ -329,7 +329,7 @@
         rate = d * old[4:5] + value[1:2]
         e = (own[5:6] - SHIFT_E + TIME_STEP * own[7:8] + scale * inflow) / (1.0 + scale * rate)
         if sweep == SWEEPS - 1:
-            energy_ref[pl.ds(s, 1), :] = e + SHIFT_E
+            out_ref[0, pl.ds(s, 1), :] = e + SHIFT_E
         else:
             en[sweep + 1, edge + s] = e
             limiter_rows(sweep + 1, edge + s)
@@ -400,11 +400,11 @@
         halos = 2 + 2 * SWEEPS - 1
         vmem = pl.BlockSpec(memory_space=pltpu.VMEM)
         smem = pl.BlockSpec(memory_space=pltpu.SMEM)
-        energy, density = pl.pallas_call(
+        both = pl.pallas_call(
             functools.partial(kernel, groups, members, tc, nb, cap),
-            out_shape=[jax.ShapeDtypeStruct((tc, TILE), F32)] * 2,
+            out_shape=jax.ShapeDtypeStruct((2, tc, TILE), F32),
             in_specs=[vmem, smem, smem, smem],
-            out_specs=[vmem, vmem],
+            out_specs=vmem,
             scratch_shapes=[
                 pltpu.VMEM((groups, cap + 1, 8, TILE), F32),
                 pltpu.VMEM((groups, cap + 1, 8, TILE), F32),
@@ -430,7 +430,7 @@
                 collective_id=0, has_side_effects=True, vmem_limit_bytes=60 * 1024 * 1024
             ),
         )(particles, new_slot, neighbours.T, ghosts)
-        return energy.reshape(-1), density.reshape(-1)
+        return both[0].reshape(-1), both[1].reshape(-1)
 
     in_specs = (
         P(None, ("group", "member")),

time: 40.9 us -> 40.4 us (0.988)
  local copies, waits for them, and re-layouts: 1.9 us -> 1.32 us
    unnamed x4 -> x0, local copies, waits for them, and re-layouts: 1.9 us -> none
    another operation x0 -> x1, local copies, waits for them, and re-layouts: none -> 1.32 us  [local(): return (both[0].reshape(-1), both[1].reshape(-1))]
where the time goes in v5:
time: 40.4 us; the launch traced here: 40.1 us
  Pallas kernels  38.2 us (95%)
  local copies, waits for them, and re-layouts  1.32 us (3%)
  between operations  0.64 us (2%)
    pallas_call x1, Pallas kernels, local(): pl.pallas_call(functools.partial(kernel, groups, members, tc, nb, cap), o...  38.2 us
    another operation x1, local copies, waits for them, and re-layouts, local(): return (both[0].reshape(-1), both[1].reshape(-1))  1.32 us

profile of v5, /device:TPU:7, one launch (start us, length us, event | category | flops | bytes accessed | tf_op | source)
XLA Modules:
  0.0 40.1 jit_solution(1976223134941113069)
XLA Ops:
  0.6 38.2 %shard_map.59 = f32[2,16,128]{2,1,0:T(8,128)} custom-call(f32[8,2048]{1,0:T(8,128)} %part_ref.1, s32[16]{0:T(128)} %slot_ref.1, s32[6,16]{1,0:T(8,128)} %bitcast.5, s32[1,2]{1,0:T(1,128)} %ghost_ref.1), custom_call_target="tpu_custom_call" | custom-call | tf_op jit(solution)/shard_map/pallas_call | solution.py:403
  38.8 1.3 %slice_bitcast_fusion = (f32[2048]{0:T(1024)}, f32[2048]{0:T(1024)}) fusion(f32[2,16,128]{2,1,0:T(8,128)} %shard_map.59), kind=kLoop, calls=%fused_computation | loop fusion | bytes 32768 | tf_op jit(solution)/shard_map/reshape;squeeze | solution.py:433
